TPU v7x, 768 devices: a whole 4x8x12 slice. The times are simulated.
768 devices in a mesh: node: 16 (over y, x_lo), feat: 48 (over z, x_hi, core).
Axes of the slice: x: 4 (x_hi: 2, x_lo: 2; x = x_hi * 2 + x_lo), y: 8, z: 12, core: 2. Of those that a mesh axis runs over, the one named last changes fastest.
Arguments:
- feats: bfloat16 [98304, 256], P(('node', 'feat')), may hold values from -6 to 6
- tile_values: bfloat16 [768, 144, 128, 128], P('node', 'feat'), may hold values from 0.049804688 to 1
- source_group: int32 [768, 144], P('node', 'feat'), may hold values from 0 to 15
- live_slots: int32 [768, 48], P('node', 'feat'), may hold values from 1 to 3, as said below
- proj_weight: bfloat16 [256, 256], replicated, may hold values from -0.375 to 0.375
- proj_bias: float32 [256], replicated, may hold values from -3 to 3
Outputs:
- updated: bfloat16 [98304, 256], P(('node', 'feat'))
Inputs may be any that keep to these rules, and one draw needn't show every extreme that they name: `live_slots`: some tile row has all 3 slots live in some column block; slots at or past the count are not part of A.
All inputs are finite; a program needn't handle non-finite values.
Results may differ from a plain program's by a relative error of at most 0.0028.
Values may be sent and summed in bfloat16 or wider, within the bound.
A program may use at most 32 MiB of HBM per device.

v0:
```python
import math

import jax
import jax.numpy as jnp
from jax import lax
from jax.sharding import PartitionSpec as P


def degrees(tiles, live_count):
    slot_index = jnp.arange(tiles.shape[1], dtype=jnp.int32)
    keep_slot = slot_index[None, :] < live_count
    per_row = jnp.sum(tiles, axis=3, dtype=jnp.float32)
    per_row = jnp.where(keep_slot[:, :, None], per_row, jnp.zeros_like(per_row))
    return jnp.sum(per_row, axis=1).reshape(-1)


def aggregate_rows(tiles, sources, live_count, source_rows):
    tile_size = source_rows.shape[1]
    width = source_rows.shape[2]
    row_count = tiles.shape[0]
    block_rows = math.gcd(row_count, 8)
    block_count = row_count // block_rows
    slot_index = jnp.arange(tiles.shape[1], dtype=jnp.int32)

    def one_block(block_args):
        block_tiles, block_sources, block_live = block_args
        keep_slot = slot_index[None, :] < block_live
        adjacency = jnp.where(keep_slot[:, :, None, None], block_tiles, jnp.zeros_like(block_tiles))
        gathered = jnp.take(source_rows, block_sources, axis=0)
        return jnp.einsum("rsab,rsbf->raf", adjacency, gathered, preferred_element_type=jnp.float32)

    block_args = (
        tiles.reshape((block_count, block_rows) + tiles.shape[1:]),
        sources.reshape(block_count, block_rows, -1),
        live_count.reshape(block_count, block_rows, -1),
    )
    products = lax.map(one_block, block_args)
    return products.reshape(row_count * tile_size, width)


def body(feats, tile_values, source_group, live_slots, proj_weight, proj_bias):
    tile_size = feats.shape[0]
    width = feats.shape[1]
    gathered = lax.all_gather(feats, "node", axis=0, tiled=True)
    source_rows = gathered.reshape(-1, tile_size, width)
    partials = aggregate_rows(tile_values, source_group, live_slots, source_rows)
    aggregate, degree_sum = (
        lax.psum_scatter(partials, "feat", scatter_dimension=0, tiled=True),
        lax.psum_scatter(degrees(tile_values, live_slots), "feat", scatter_dimension=0, tiled=True),
    )
    own_rows = feats.astype(jnp.float32)
    inv_root = lax.rsqrt(degree_sum + 1.0)
    normed = ((aggregate + own_rows) * inv_root[:, None]).astype(jnp.bfloat16)
    hidden = jnp.dot(normed, proj_weight, preferred_element_type=jnp.float32) + proj_bias
    return (own_rows + jax.nn.relu(hidden)).astype(jnp.bfloat16)


def solution(mesh):
    placed = (
        P(("node", "feat"), None),
        P("node", "feat", None, None),
        P("node", "feat"),
        P("node", "feat"),
        P(),
        P(),
    )
    return jax.shard_map(
        body, mesh=mesh, in_specs=placed, out_specs=P(("node", "feat"), None), check_vma=False
    )
```

profile of v0, /device:TPU:1, one launch (start us, length us, event | category | flops | bytes accessed | tf_op | source)
XLA Modules:
  0.0 324.6 jit_solution(16092467928925218750)
XLA Ops:
  6.5 0.7 all-gather.2.cloned.1.call-update
  7.3 0.6 broadcast.81
  7.9 1.4 reduce.3
  9.4 0.8 reshape.108
  10.1 71.4 %all-gather.2.cloned.1.call-done = bf16[2048,256]{1,0:T(8,128)(2,1)} async-done(((bf16[128,256]{1,0:T(8,128)(2,1)}), bf16[2048,256]{1,0:T(8,128)(2,1)}) %all-gather.2.cloned.1.call-update) | async-done | bytes 1048592 | tf_op jit(solution)/shard_map/all_gather | solution.py:44
  81.5 29.5 %while.11 = (s32[]{:T(128)}, f32[6,8,128,256]{3,2,1,0:T(8,128)}, s32[6,8,1]{1,2,0:T(1,128)S(1)}, bf16[6,8,3,128,128]{4,3,2,1,0:T(8,128)(2,1)}, s32[6,8,3]{1,0,2:...) while((s32[]{:T(128)}, f32[6,8,128,256]{3,2,1,0:T(8,128)}, s32[6,8,1]{1,2,0:T(1,128)S(1)}, ...), condition=%wide.region_1.2_spmd.clone, body=%wide.region_0.1_spmd.clone.sunk | while | flops 202507504 | bytes 6560005 | solution.py:37
  81.7 1.9 gather_fusion
  83.8 2.7 fusion.33
  86.6 1.9 gather_fusion
  88.5 0.1 copy.34
  88.7 2.7 fusion.33
  91.5 1.9 gather_fusion
  93.6 2.6 fusion.33
  96.4 1.9 gather_fusion
  98.5 2.6 fusion.33
  101.3 1.9 gather_fusion
  103.4 2.6 fusion.33
  106.2 1.9 gather_fusion
  108.3 2.7 fusion.33
  111.0 1.3 dynamic-slice
  113.1 3.7 %convert_reduce_fusion = f32[48,3,128]{2,1,0:T(4,128)S(1)} fusion(bf16[48,3,128,128]{3,2,1,0:T(8,128)(2,1)} %bitcast.46), kind=kLoop, calls=%fused_computation.23 | loop fusion | flops 4700160 | bytes 4792320 | tf_op jit(solution)/shard_map/reduce_sum | solution.py:12
  116.7 0.1 select_reduce_fusion
  116.9 199.0 %all-reduce = f32[6144]{0:T(1024)S(1)} all-reduce(f32[6144]{0:T(1024)S(1)} %bitcast.47), channel_id=3, replica_groups=mesh['node'=16,'feat'=48] {'feat'}, use_global_device_ids=true, to_apply=%region_5.6.clone | all-reduce | flops 6144 | bytes 49152
  316.0 1.8 fusion.21
  (63 shorter events, 2.4 us)
Async XLA Ops:
  6.5 309.5 %copy-start = (bf16[256,256]{1,0:T(8,128)(2,1)S(1)}, bf16[256,256]{1,0:T(8,128)(2,1)}, u32[]{:S(2)}) copy-start(bf16[256,256]{1,0:T(8,128)(2,1)} %param.12) | copy-start | bytes 393220
  6.5 75.0 %all-gather.2.cloned.1.call-start = ((), (), s32[]{:S(2)}) async-start(), calls=%async_computation.1 | async-start | bytes 1114112 | tf_op jit(solution)/shard_map/all_gather | solution.py:44
  7.3 308.7 %reduce-scatter.2.cloned.1.call-start = ((), (), s32[]{:S(2)}) async-start(), calls=%async_computation.2 | async-start | bytes 6422528 | tf_op jit(solution)/shard_map/reduce_scatter | solution.py:48
  111.0 2.0 copy-start.3
  111.0 205.0 %copy-start.1 = (bf16[128,256]{1,0:T(8,128)(2,1)S(1)}, bf16[128,256]{1,0:T(8,128)(2,1)}, u32[]{:S(2)}) copy-start(bf16[128,256]{1,0:T(8,128)(2,1)} %param.8) | copy-start | bytes 196612
  111.0 205.0 %copy-start.2 = (f32[256]{0:T(256)S(1)}, f32[256]{0:T(256)}, u32[]{:S(2)}) copy-start(f32[256]{0:T(256)} %param.13) | copy-start | bytes 3076
Sparse Core Ops, SparseCore 0:
  9.7 71.7 all-gather.1
  111.1 196.7 reduce-scatter.1
where the time goes:
time: 329 us; the launch traced here: 325 us
  blocking collectives  199 us (60%)
  waiting for transfers between devices  72.1 us (22%)
  matrix products  17.7 us (5%)
  local copies, waits for them, and re-layouts  15.6 us (5%)
  between operations  14.1 us (4%)
  other arithmetic  5.92 us (2%)
    unnamed x1, blocking collectives  199 us
    all_gather x1, waiting for transfers between devices, body(): gathered = lax.all_gather(feats, 'node', axis=0, tiled=True)  71.4 us
    dot_general x6, matrix products, one_block(): jnp.einsum('rsab,rsbf->raf', adjacency, gathered, preferred_element_type=...  16 us
    gather x6, local copies, waits for them, and re-layouts, one_block(): gathered = jnp.take(source_rows, block_sources, axis=0)  11.2 us
  transfers between devices with their start and end apart: 2, of which 1 were waited for; matrix products, arithmetic and copies ran while one was open for 2% of the time, Pallas kernels for 0%

commit v1 on v0

v1 whole, which is shorter than its diff:
```python
import jax
import jax.numpy as jnp
from jax import lax
from jax.experimental import pallas as pl
from jax.experimental.pallas import tpu as pltpu
from jax.sharding import PartitionSpec as P

SLOTS = 3
MESH = pl.DeviceIdType.MESH
F32 = jnp.float32
BF16 = jnp.bfloat16


def make_kernel(ny, nz):
    nodes = 2 * ny
    feats_n = 4 * nz
    half = nz // 2
    yhalf = ny // 2
    last = nz - 1

    def kernel(feats, tiles_hbm, src, live, weight, bias, out,
               tiles, fbuf, own, psend, precv, rsend, rrecv, xsend, xrecv,
               dmat, dpair, dsend, drecv, dxsend, dxrecv,
               tsem, ag_s, ag_r, p_s, p_r, r_s, r_r, x_s, x_r,
               dp_s, dp_r, dr_s, dr_r, dx_s, dx_r):
        n = lax.axis_index("node")
        f = lax.axis_index("feat")
        z = f // 4
        h = (f // 2) % 2
        c = f % 2
        n_x = n + 1 - 2 * (n % 2)
        n_up = (n + 2) % nodes
        n_dn = (n + nodes - 2) % nodes
        f_core = f + 1 - 2 * c
        f_opp = f + 2 - 4 * h
        f_up = (f + 4) % feats_n
        f_dn = (f + feats_n - 4) % feats_n

        rows_n = tiles_hbm.shape[0]
        parts = tsem.shape[0]
        step_rows = rows_n // parts

        def tile_copy(i):
            sl = pl.ds(i * step_rows, step_rows)
            return pltpu.make_async_copy(tiles_hbm.at[sl], tiles.at[sl], tsem.at[i])

        for i in range(parts):
            tile_copy(i).start()

        barrier = pltpu.get_barrier_semaphore()
        for dev in (dict(node=n_x), dict(node=n_up), dict(node=n_dn)):
            pl.semaphore_signal(barrier, inc=1, device_id=dict(node=dev["node"], feat=f), device_id_type=MESH)
        for fd in (f_core, f_opp, f_up, f_dn):
            pl.semaphore_signal(barrier, inc=1, device_id=dict(node=n, feat=fd), device_id_type=MESH)
        pl.semaphore_wait(barrier, 7)

        def remote(s, d, ss, rs, node=None, feat=None):
            dev = dict(node=n if node is None else node, feat=f if feat is None else feat)
            return pltpu.make_async_remote_copy(
                src_ref=s, dst_ref=d, send_sem=ss, recv_sem=rs, device_id=dev, device_id_type=MESH)

        def ag(way, block, source=None):
            dest = (n_x, n_up, n_dn)[way]
            s = fbuf.at[block] if source is None else source
            return remote(s, fbuf.at[block], ag_s.at[way, block], ag_r.at[block], node=dest)

        ag(0, n, feats).start()
        ag(1, n, feats).start()
        ag(2, n, feats).start()

        fbuf[n] = feats[...]
        fbuf[nodes] = jnp.zeros_like(feats)

        for i in range(parts):
            tile_copy(i).wait()
        lane = lax.broadcasted_iota(jnp.int32, (128, 128), 1)

        def degree_row(r, d):
            total = jnp.zeros((128, 128), F32)
            count = live[r, 0]
            for s in range(SLOTS):
                on = jnp.where(count > s, 1.0, 0.0).astype(F32)
                total = total + tiles[r, s].astype(F32) * on
            rowsum = jnp.sum(total, axis=1, keepdims=True)
            return jnp.where(lane == 8 * (r // 4) + r % 4, rowsum, d)

        d = lax.fori_loop(0, rows_n, degree_row, jnp.zeros((128, 128), F32))
        dmat[...] = d.T.reshape(16, 8, 128)
        dpc = remote(dmat, dpair, dp_s, dp_r, feat=f_core)
        dpc.start()

        ag(0, n_x).wait_recv()
        ag(1, n_x).start()
        ag(2, n_x).start()
        for dist in range(1, yhalf + 1):
            for base, way, reach in ((n, 1, yhalf), (n, 2, yhalf - 1), (n_x, 1, yhalf - 1), (n_x, 2, yhalf)):
                if dist > reach:
                    continue
                if way == 1:
                    block = (base + nodes - 2 * dist) % nodes
                else:
                    block = (base + 2 * dist) % nodes
                ag(way, block).wait_recv()
                if dist + 1 <= reach:
                    ag(way, block).start()

        def compute(u, carry):
            off = jnp.where(u % 2 == 1, half - (u + 1) // 2, half + u // 2)
            zt = (z + off) % nz

            def product(ht, ct):
                r = 4 * zt + 2 * ht + ct
                count = live[r, 0]
                a = jnp.concatenate([tiles[r, s] for s in range(SLOTS)], axis=1)
                b = jnp.concatenate(
                    [fbuf[jnp.where(count > s, src[r, s], nodes)] for s in range(SLOTS)], axis=0)
                return jnp.dot(a, b, preferred_element_type=F32)

            for ht in range(2):
                psend[u, ht] = product(ht, 1 - c).astype(BF16)
            pair(u).start()
            for ht in range(2):
                own[u, ht] = product(ht, c)
            return carry

        def pair(u):
            return remote(psend.at[u], precv.at[u], p_s.at[u], p_r.at[u], feat=f_core)

        is_up = (True, False, True, False)
        col = (0, 1, 1, 0)

        def ring(s, k):
            return remote(rsend.at[s, k], rrecv.at[s, k], r_s.at[s, k], r_r.at[s, k],
                          feat=f_up if is_up[s] else f_dn)

        def dring(way, k):
            return remote(dsend.at[way, k], drecv.at[way, k], dr_s.at[way, k], dr_r.at[way, k],
                          feat=f_dn if way else f_up)

        def ring_step(k, streams, incoming, first):
            for s in streams:
                u = 0 if first else (2 * k - 1 if is_up[s] else 2 * k)
                cs = slice(col[s] * 128, col[s] * 128 + 128)
                if s in incoming:
                    ring(s, k - 1).wait_recv()
                for ht in range(2):
                    v = own[u, ht, :, cs] + precv[u, ht, :, cs].astype(F32)
                    if s in incoming:
                        v = v + rrecv[s, k - 1, ht].astype(F32)
                    rsend[s, k, ht] = v.astype(BF16)
                ring(s, k).start()

        def dstep(k, ways, incoming):
            for way in ways:
                zt = (z + half - k) % nz if way == 0 else (z + half + k) % nz
                v = dmat[zt]
                if way in incoming:
                    dring(way, k - 1).wait_recv()
                    v = v + drecv[way, k - 1]
                dsend[way, k] = v
                dring(way, k).start()

        lax.fori_loop(0, 3, compute, 0)
        dpc.wait()
        dmat[...] = dmat[...] + dpair[...]
        pair(0).wait_recv()
        ring_step(0, (0, 1), (), True)
        dstep(0, (0,), ())
        pair(1).wait_recv()
        pair(2).wait_recv()
        ring_step(1, (0, 1, 2, 3), (0, 1), False)
        dstep(1, (0, 1), (0,))
        lax.fori_loop(3, 5, compute, 0)

        def mid(k, carry):
            pair(2 * k - 1).wait_recv()
            pair(2 * k).wait_recv()
            ring_step(k, (0, 1, 2, 3), (0, 1, 2, 3), False)
            dstep(k, (0, 1), (0, 1))
            lax.fori_loop(2 * k + 1, jnp.minimum(2 * k + 3, nz), compute, 0)
            return carry

        lax.fori_loop(2, half, mid, 0)

        pair(last).wait_recv()
        e = half - 1

        def total(ht):
            left = own[last, ht, :, 0:128] + precv[last, ht, :, 0:128].astype(F32)
            left = left + rrecv[0, e, ht].astype(F32) + rrecv[3, e, ht].astype(F32)
            right = own[last, ht, :, 128:256] + precv[last, ht, :, 128:256].astype(F32)
            right = right + rrecv[1, e, ht].astype(F32) + rrecv[2, e, ht].astype(F32)
            return left, right

        dring(0, e).wait_recv()
        dring(1, e).wait_recv()
        dxsend[...] = dmat[z] + drecv[0, e] + drecv[1, e]
        dxc = remote(dxsend, dxrecv, dx_s, dx_r, feat=f_opp)
        dxc.start()
        for s in range(4):
            ring(s, e).wait_recv()
        left, right = total(1 - h)
        xsend[:, 0:128] = left.astype(BF16)
        xsend[:, 128:256] = right.astype(BF16)
        xc = remote(xsend, xrecv, x_s, x_r, feat=f_opp)
        xc.start()
        left, right = total(h)
        mine = feats[...].astype(F32)
        agg = jnp.concatenate([left, right], axis=1) + mine

        dxc.wait_recv()
        drow = dxsend[pl.ds(2 * h + c, 1), :] + dxrecv[pl.ds(2 * h + c, 1), :] + 1.0
        inv = lax.rsqrt(jnp.broadcast_to(drow, (128, 128)).T)
        inv = jnp.concatenate([inv, inv], axis=1)
        xc.wait_recv()
        normed = ((agg + xrecv[...].astype(F32)) * inv).astype(BF16)
        hidden = jnp.dot(normed, weight[...], preferred_element_type=F32) + bias[...]
        out[...] = (mine + jnp.maximum(hidden, 0.0)).astype(BF16)

        xc.wait_send()
        dxc.wait_send()
        ag(0, n, feats).wait_send()
        ag(1, n, feats).wait_send()
        ag(2, n, feats).wait_send()
        ag(1, n_x).wait_send()
        ag(2, n_x).wait_send()
        for dist in range(1, yhalf):
            for base, way, reach in ((n, 1, yhalf), (n, 2, yhalf - 1), (n_x, 1, yhalf - 1), (n_x, 2, yhalf)):
                if dist + 1 > reach:
                    continue
                if way == 1:
                    block = (base + nodes - 2 * dist) % nodes
                else:
                    block = (base + 2 * dist) % nodes
                ag(way, block).wait_send()

        def drain_pair(u, carry):
            pair(u).wait_send()
            return carry

        lax.fori_loop(0, nz, drain_pair, 0)

        def drain_ring(k, carry):
            for s in range(4):
                ring(s, k).wait_send()
            dring(0, k).wait_send()
            dring(1, k).wait_send()
            return carry

        ring(0, 0).wait_send()
        ring(1, 0).wait_send()
        dring(0, 0).wait_send()
        lax.fori_loop(1, half, drain_ring, 0)

    return kernel


def make_body(ny, nz):
    nodes = 2 * ny
    half = nz // 2
    dma = pltpu.SemaphoreType.DMA
    vmem = pl.BlockSpec(memory_space=pltpu.VMEM)
    smem = pl.BlockSpec(memory_space=pltpu.SMEM)

    def body(feats, tile_values, source_group, live_slots, proj_weight, proj_bias):
        rows_n = tile_values.shape[0]
        scratch = [
            pltpu.VMEM((rows_n, SLOTS, 128, 128), BF16),
            pltpu.VMEM((nodes + 1, 128, 256), BF16),
            pltpu.VMEM((nz, 2, 128, 256), F32),
            pltpu.VMEM((nz, 2, 128, 256), BF16),
            pltpu.VMEM((nz, 2, 128, 256), BF16),
            pltpu.VMEM((4, half, 2, 128, 128), BF16),
            pltpu.VMEM((4, half, 2, 128, 128), BF16),
            pltpu.VMEM((128, 256), BF16),
            pltpu.VMEM((128, 256), BF16),
            pltpu.VMEM((16, 8, 128), F32),
            pltpu.VMEM((16, 8, 128), F32),
            pltpu.VMEM((2, half, 8, 128), F32),
            pltpu.VMEM((2, half, 8, 128), F32),
            pltpu.VMEM((8, 128), F32),
            pltpu.VMEM((8, 128), F32),
            dma((6,)),
            dma((3, nodes)), dma((nodes,)),
            dma((nz,)), dma((nz,)),
            dma((4, half)), dma((4, half)),
            dma, dma,
            dma, dma,
            dma((2, half)), dma((2, half)),
            dma, dma,
        ]
        return pl.pallas_call(
            make_kernel(ny, nz),
            out_shape=jax.ShapeDtypeStruct(feats.shape, BF16),
            in_specs=[vmem, pl.BlockSpec(memory_space=pl.ANY), smem, smem, vmem, vmem],
            out_specs=vmem,
            scratch_shapes=scratch,
            compiler_params=pltpu.CompilerParams(
                collective_id=0, has_side_effects=True, vmem_limit_bytes=60 << 20),
            name="graph_layer",
        )(feats, tile_values, source_group, live_slots, proj_weight, proj_bias.reshape(1, -1))

    return body


def solution(mesh):
    placed = (
        P(("node", "feat"), None),
        P("node", "feat", None, None),
        P("node", "feat"),
        P("node", "feat"),
        P(),
        P(),
    )
    return jax.shard_map(
        make_body(mesh.shape["node"] // 2, mesh.shape["feat"] // 4),
        mesh=mesh, in_specs=placed, out_specs=P(("node", "feat"), None), check_vma=False,
    )
```

time: 329 us -> 75.6 us (0.23); the launches traced: 325 us -> 74.7 us
  blocking collectives: 199 us -> 0 us
  waiting for transfers between devices: 72.1 us -> 0 us
  Pallas kernels: 0 us -> 70.5 us
  matrix products: 17.7 us -> 0 us
  between operations: 14.1 us -> 0.01 us
  local copies, waits for them, and re-layouts: 15.6 us -> 4.18 us
  other arithmetic: 5.92 us -> 0 us
    unnamed x1 -> x0, blocking collectives: 199 us -> none
    all_gather x1 -> x0, waiting for transfers between devices: 71.4 us -> none  [body(): gathered = lax.all_gather(feats, 'node', axis=0, tiled=True)]
    pallas_call x0 -> x1, Pallas kernels: none -> 70.5 us  [body(): pl.pallas_call(make_kernel(ny, nz), out_shape=jax.ShapeDtypeStruct(feats....]
    dot_general x7 -> x0, matrix products: 17.7 us -> none  [the longest x6 16 us: one_block(): jnp.einsum('rsab,rsbf->raf', adjacency, gathered, preferred_element_type=...]
    gather x6 -> x0, local copies, waits for them, and re-layouts: 11.2 us -> none  [one_block(): gathered = jnp.take(source_rows, block_sources, axis=0)]
    reduce_sum x2 -> x0, other arithmetic: 3.82 us -> none  [the longest x1 3.67 us: degrees(): per_row = jnp.sum(tiles, axis=3, dtype=jnp.float32)]
  transfers between devices with their start and end apart: 2 -> 0, of which waited for: 1 -> 0; matrix products, arithmetic and copies ran while one was open for 2% -> 0% of each run, Pallas kernels for 0% -> 0%
where the time goes in v1:
time: 75.6 us; the launch traced here: 74.7 us
  Pallas kernels  70.5 us (93%)
  local copies, waits for them, and re-layouts  4.18 us (6%)
    pallas_call x1, Pallas kernels, body(): pl.pallas_call(make_kernel(ny, nz), out_shape=jax.ShapeDtypeStruct(feats....  70.5 us
    unnamed x3, local copies, waits for them, and re-layouts  4.18 us

profile of v1, /device:TPU:1, one launch (start us, length us, event | category | flops | bytes accessed | tf_op | source)
XLA Modules:
  0.0 74.7 jit_solution(6103820859847895803)
XLA Ops:
  0.0 1.4 %copy.7.src = s32[48,3]{1,0:T(8,128)} copy(s32[48,3]{0,1:T(4,128)} %param.8) | data formatting | bytes 1152 | tf_op args[2]
  1.4 1.3 %copy.8.live = s32[48,1]{1,0:T(8,128)} copy(s32[48,1]{0,1:T(1,128)} %param.9) | data formatting | bytes 384 | tf_op args[3]
  2.7 70.5 %graph_layer.1 = bf16[128,256]{1,0:T(8,128)(2,1)} custom-call(bf16[128,256]{1,0:T(8,128)(2,1)} %feats.1, bf16[48,3,128,128]{3,2,1,0:T(8,128)(2,1)} %tiles_hbm.1, s32[48,3]{1,0:T(8,128)} %copy.7.src, s32[48,1]{1,0:T(8,128)} %copy.8.live, bf16[256,256]{1,0:T(8,128)(2,1)} %weight.1, f32[1,256]{1,0:T(1,128)} %bitcast.1), custom_call_target="tpu_custom_call" | custom-call | tf_op jit(solution)/shard_map/graph_layer/pallas_call | solution.py:292
  73.2 1.5 %copy.10 = bf16[128,256]{1,0:T(8,128)(2,1)} copy(bf16[128,256]{1,0:T(8,128)(2,1)} %graph_layer.1) | data formatting | bytes 131072

commit v2 on v1

v2 whole, which is shorter than its diff:
```python
import jax
import jax.numpy as jnp
from jax import lax
from jax.experimental import pallas as pl
from jax.experimental.pallas import tpu as pltpu
from jax.sharding import PartitionSpec as P

SLOTS = 3
MESH = pl.DeviceIdType.MESH
F32 = jnp.float32
BF16 = jnp.bfloat16


def make_kernel(ny, nz):
    nodes = 2 * ny
    feats_n = 4 * nz
    half = nz // 2
    yhalf = ny // 2
    last = nz - 1

    def kernel(feats, tiles_hbm, src, live, weight, bias, out,
               tiles, fbuf, own, psend, precv, rsend, rrecv, xsend, xrecv,
               dloc, dsend, drecv, dtot, dxrecv,
               tsem, own_s, ag_s, ag_r, p_s, p_r, r_s, r_r, x_s, x_r,
               dr_s, dr_r, dx_s, dx_r):
        n = lax.axis_index("node")
        f = lax.axis_index("feat")
        z = f // 4
        h = (f // 2) % 2
        c = f % 2
        n_x = n + 1 - 2 * (n % 2)
        n_up = (n + 2) % nodes
        n_dn = (n + nodes - 2) % nodes
        f_core = f + 1 - 2 * c
        f_opp = f + 2 - 4 * h
        f_up = (f + 4) % feats_n
        f_dn = (f + feats_n - 4) % feats_n

        rows_n = tiles_hbm.shape[0]
        parts = tsem.shape[0]
        step_rows = rows_n // parts

        def tile_copy(i):
            sl = pl.ds(i * step_rows, step_rows)
            return pltpu.make_async_copy(tiles_hbm.at[sl], tiles.at[sl], tsem.at[i])

        for i in range(parts):
            tile_copy(i).start()

        barrier = pltpu.get_barrier_semaphore()
        near = [(nd, f) for nd in (n_x, n_up, n_dn, (n_x + 2) % nodes, (n_x + nodes - 2) % nodes)]
        near += [(n, fd) for fd in (f_core, f_opp, f_opp + 1 - 2 * c, f_up, f_dn)]
        for nd, fd in near:
            pl.semaphore_signal(barrier, inc=1, device_id=dict(node=nd, feat=fd), device_id_type=MESH)
        pl.semaphore_wait(barrier, len(near))

        def remote(s, d, ss, rs, node=None, feat=None):
            dev = dict(node=n if node is None else node, feat=f if feat is None else feat)
            return pltpu.make_async_remote_copy(
                src_ref=s, dst_ref=d, send_sem=ss, recv_sem=rs, device_id=dev, device_id_type=MESH)

        def block_at(base, way, dist):
            return (base + nodes - 2 * dist) % nodes if way == 0 else (base + 2 * dist) % nodes

        def ag(way, block, q):
            ref = fbuf.at[block, pl.ds(64 * q, 64)]
            return remote(ref, ref, ag_s.at[block, q], ag_r.at[block, q], node=n_dn if way else n_up)

        def ag_own(i, q):
            dest = (n_up, n_dn, n_x, (n_x + 2) % nodes, (n_x + nodes - 2) % nodes)[i]
            return remote(feats.at[pl.ds(64 * q, 64)], fbuf.at[n, pl.ds(64 * q, 64)],
                          own_s.at[i, q], ag_r.at[n, q], node=dest)

        hops = []
        for dist in range(1, yhalf + 1):
            for side in range(2):
                for q in range(2):
                    for way in range(2):
                        reach = yhalf if way == q else yhalf - 1
                        if dist <= reach:
                            hops.append((side, way, q, dist, dist < reach))

        for i in (0, 1, 3, 4, 2):
            for q in range(2):
                ag_own(i, q).start()

        fbuf[n] = feats[...]
        fbuf[nodes] = jnp.zeros_like(feats)
        dloc[...] = jnp.zeros_like(dloc)

        for side, way, q, dist, onward in hops:
            block = block_at(n_x if side else n, way, dist)
            ag(way, block, q).wait_recv()
            if onward:
                ag(way, block, q).start()
        for q in range(2):
            ag(0, n_x, q).wait_recv()
        for i in range(parts):
            tile_copy(i).wait()

        slot_of = lax.broadcasted_iota(jnp.int32, (16, SLOTS * 128), 1) // 128

        def pair(u):
            return remote(psend.at[u], precv.at[u], p_s.at[u], p_r.at[u], feat=f_core)

        def group(u, j):
            off = jnp.where(u % 2 == 1, half - (u + 1) // 2, half + u // 2)
            zt = (z + off) % nz
            ht = j % 2
            ct = 1 - c if j < 2 else c
            r = 4 * zt + 2 * ht + ct
            count = live[0, r]
            a = jnp.concatenate([tiles[r, s] for s in range(SLOTS)], axis=1)
            b = jnp.concatenate(
                [fbuf[jnp.where(count > s, src[s, r], nodes)] for s in range(SLOTS)], axis=0)
            on = jnp.where(slot_of < count, 1.0, 0.0).astype(BF16)
            got = jnp.dot(a, b, preferred_element_type=F32)
            rowsum = lax.dot_general(on, a, (((1,), (1,)), ((), ())), preferred_element_type=F32)
            dloc[u, pl.ds(2 * ht + ct, 1), :] = rowsum[0:1, :]
            if j < 2:
                psend[u, ht] = got.astype(BF16)
            else:
                own[u, ht] = got
            if j == 1:
                pair(u).start()

        streams = ((0, 0, 0), (1, 1, 0), (0, 0, 1), (1, 1, 1), (0, 1, 0), (1, 0, 0), (0, 1, 1), (1, 0, 1))
        far = streams[:4]

        def ring(s, k):
            w, q, ht = s
            return remote(rsend.at[w, q, ht, k], rrecv.at[w, q, ht, k], r_s.at[w, q, ht, k], r_r.at[w, q, ht, k],
                          feat=f_dn if w else f_up)

        def dring(w, k):
            return remote(dsend.at[w, k], drecv.at[w, k], dr_s.at[w, k], dr_r.at[w, k],
                          feat=f_dn if w else f_up)

        def ring_step(k, active, incoming, first, todo):
            todo = list(todo)
            for s in active:
                w, q, ht = s
                u = 0 if first else 2 * k - 1 + w
                cs = slice(q * 128, q * 128 + 128)
                if s in incoming:
                    ring(s, k - 1).wait_recv()
                v = own[u, ht, :, cs] + precv[u, ht, :, cs].astype(F32)
                if s in incoming:
                    v = v + rrecv[w, q, ht, k - 1].astype(F32)
                rsend[w, q, ht, k] = v.astype(BF16)
                ring(s, k).start()
                if todo:
                    group(*todo.pop(0))
            for t in todo:
                group(*t)

        def dstep(k, ways, incoming, first):
            for w in ways:
                v = dloc[0 if first else 2 * k - 1 + w]
                if w in incoming:
                    dring(w, k - 1).wait_recv()
                    v = v + drecv[w, k - 1]
                dsend[w, k] = v
                dring(w, k).start()

        def ahead(k):
            return [(u, j) for u in (2 * k + 2, 2 * k + 3) for j in range(4)]

        def begin(u, carry):
            for j in range(4):
                group(u, j)
            return carry

        lax.fori_loop(0, 2, begin, 0)
        pair(0).wait_recv()
        ring_step(0, far, (), True, ())
        dstep(0, (0,), (), True)
        lax.fori_loop(2, 4, begin, 0)
        pair(1).wait_recv()
        pair(2).wait_recv()
        ring_step(1, streams, far, False, ahead(1))
        dstep(1, (0, 1), (0,), False)

        def mid(k, carry):
            pair(2 * k - 1).wait_recv()
            pair(2 * k).wait_recv()
            ring_step(k, streams, streams, False, ahead(k))
            dstep(k, (0, 1), (0, 1), False)
            return carry

        lax.fori_loop(2, half - 1, mid, 0)
        e = half - 1
        pair(2 * e - 1).wait_recv()
        pair(2 * e).wait_recv()
        ring_step(e, streams, streams, False, ())
        dstep(e, (0, 1), (0, 1), False)
        pair(last).wait_recv()

        def total(ht, q):
            cs = slice(q * 128, q * 128 + 128)
            v = own[last, ht, :, cs] + precv[last, ht, :, cs].astype(F32)
            for w in range(2):
                ring((w, q, ht), e).wait_recv()
                v = v + rrecv[w, q, ht, e].astype(F32)
            return v

        def xc(q):
            return remote(xsend.at[q], xrecv.at[q], x_s.at[q], x_r.at[q], feat=f_opp)

        def dxc(i):
            return remote(dtot, dxrecv.at[i], dx_s.at[i], dx_r.at[i],
                          feat=(f_core, f_opp, f_opp + 1 - 2 * c)[i])

        for q in range(2):
            xsend[q] = total(1 - h, q).astype(BF16)
            xc(q).start()
        dring(0, e).wait_recv()
        dring(1, e).wait_recv()
        dtot[...] = dloc[last] + drecv[0, e] + drecv[1, e]
        for i in range(3):
            dxc(i).start()
        mine = feats[...].astype(F32)
        agg = jnp.concatenate([total(h, 0), total(h, 1)], axis=1) + mine
        row = pl.ds(2 * h + c, 1)
        drow = dtot[row, :] + 1.0
        for i in range(3):
            dxc(i).wait_recv()
            drow = drow + dxrecv[i, row, :]
        inv = lax.rsqrt(jnp.broadcast_to(drow, (128, 128)).T)
        inv = jnp.concatenate([inv, inv], axis=1)
        for q in range(2):
            xc(q).wait_recv()
        agg = agg + jnp.concatenate([xrecv[0], xrecv[1]], axis=1).astype(F32)
        normed = (agg * inv).astype(BF16)
        hidden = jnp.dot(normed, weight[...], preferred_element_type=F32) + bias[...]
        out[...] = (mine + jnp.maximum(hidden, 0.0)).astype(BF16)

        for q in range(2):
            xc(q).wait_send()
            for i in range(5):
                ag_own(i, q).wait_send()
        for i in range(3):
            dxc(i).wait_send()
        for side, way, q, dist, onward in hops:
            if onward:
                ag(way, block_at(n_x if side else n, way, dist), q).wait_send()

        def drain_pair(u, carry):
            pair(u).wait_send()
            return carry

        lax.fori_loop(0, nz, drain_pair, 0)

        def drain_ring(k, carry):
            for s in streams:
                ring(s, k).wait_send()
            dring(0, k).wait_send()
            dring(1, k).wait_send()
            return carry

        for s in far:
            ring(s, 0).wait_send()
        dring(0, 0).wait_send()
        lax.fori_loop(1, half, drain_ring, 0)

    return kernel


def make_body(ny, nz):
    nodes = 2 * ny
    half = nz // 2
    dma = pltpu.SemaphoreType.DMA
    vmem = pl.BlockSpec(memory_space=pltpu.VMEM)
    smem = pl.BlockSpec(memory_space=pltpu.SMEM)

    def body(feats, tile_values, source_group, live_slots, proj_weight, proj_bias):
        rows_n = tile_values.shape[0]
        scratch = [
            pltpu.VMEM((rows_n, SLOTS, 128, 128), BF16),
            pltpu.VMEM((nodes + 1, 128, 256), BF16),
            pltpu.VMEM((nz, 2, 128, 256), F32),
            pltpu.VMEM((nz, 2, 128, 256), BF16),
            pltpu.VMEM((nz, 2, 128, 256), BF16),
            pltpu.VMEM((2, 2, 2, half, 128, 128), BF16),
            pltpu.VMEM((2, 2, 2, half, 128, 128), BF16),
            pltpu.VMEM((2, 128, 128), BF16),
            pltpu.VMEM((2, 128, 128), BF16),
            pltpu.VMEM((nz, 8, 128), F32),
            pltpu.VMEM((2, half, 8, 128), F32),
            pltpu.VMEM((2, half, 8, 128), F32),
            pltpu.VMEM((8, 128), F32),
            pltpu.VMEM((3, 8, 128), F32),
            dma((6,)),
            dma((5, 2)), dma((nodes, 2)), dma((nodes, 2)),
            dma((nz,)), dma((nz,)),
            dma((2, 2, 2, half)), dma((2, 2, 2, half)),
            dma((2,)), dma((2,)),
            dma((2, half)), dma((2, half)),
            dma((3,)), dma((3,)),
        ]
        return pl.pallas_call(
            make_kernel(ny, nz),
            out_shape=jax.ShapeDtypeStruct(feats.shape, BF16),
            in_specs=[vmem, pl.BlockSpec(memory_space=pl.ANY), smem, smem, vmem, vmem],
            out_specs=vmem,
            scratch_shapes=scratch,
            compiler_params=pltpu.CompilerParams(
                collective_id=0, has_side_effects=True, vmem_limit_bytes=60 << 20),
            name="graph_layer",
        )(feats, tile_values, source_group.T, live_slots.T, proj_weight, proj_bias.reshape(1, -1))

    return body


def solution(mesh):
    placed = (
        P(("node", "feat"), None),
        P("node", "feat", None, None),
        P("node", "feat"),
        P("node", "feat"),
        P(),
        P(),
    )
    return jax.shard_map(
        make_body(mesh.shape["node"] // 2, mesh.shape["feat"] // 4),
        mesh=mesh, in_specs=placed, out_specs=P(("node", "feat"), None), check_vma=False,
    )
```

time: 75.6 us -> 68.2 us (0.902)
  Pallas kernels: 70.5 us -> 66.5 us
  local copies, waits for them, and re-layouts: 4.18 us -> 1.47 us
    pallas_call x1, Pallas kernels: 70.5 us -> 66.5 us  [body(): pl.pallas_call(make_kernel(ny, nz), out_shape=jax.ShapeDtypeStruct(feats....]
    unnamed x3 -> x1, local copies, waits for them, and re-layouts: 4.18 us -> 1.47 us
where the time goes in v2:
time: 68.2 us; the launch traced here: 68 us
  Pallas kernels  66.5 us (98%)
  local copies, waits for them, and re-layouts  1.47 us (2%)
    pallas_call x1, Pallas kernels, body(): pl.pallas_call(make_kernel(ny, nz), out_shape=jax.ShapeDtypeStruct(feats....  66.5 us
    unnamed x1, local copies, waits for them, and re-layouts  1.47 us

profile of v2, /device:TPU:1, one launch (start us, length us, event | category | flops | bytes accessed | tf_op | source)
XLA Modules:
  0.0 68.0 jit_solution(8361395120258325973)
XLA Ops:
  0.0 66.5 %graph_layer.1 = bf16[128,256]{1,0:T(8,128)(2,1)} custom-call(bf16[128,256]{1,0:T(8,128)(2,1)} %feats.1, bf16[48,3,128,128]{3,2,1,0:T(8,128)(2,1)} %tiles_hbm.1, s32[3,48]{1,0:T(4,128)} %bitcast.3, s32[1,48]{1,0:T(1,128)} %bitcast.5, bf16[256,256]{1,0:T(8,128)(2,1)} %weight.1, f32[1,256]{1,0:T(1,128)} %bitcast.4), custom_call_target="tpu_custom_call" | custom-call | tf_op jit(solution)/shard_map/graph_layer/pallas_call | solution.py:301
  66.5 1.5 %copy.8 = bf16[128,256]{1,0:T(8,128)(2,1)} copy(bf16[128,256]{1,0:T(8,128)(2,1)} %graph_layer.1) | data formatting | bytes 131072

commit v3 on v2

v3 whole, which is shorter than its diff:
```python
import jax
import jax.numpy as jnp
from jax import lax
from jax.experimental import pallas as pl
from jax.experimental.pallas import tpu as pltpu
from jax.sharding import PartitionSpec as P

SLOTS = 3
TOP = 48
LOW = "low"
MESH = pl.DeviceIdType.MESH
HOPS = (
    (0, 0, -1, 0, 0), (0, 1, 0, 0, 0), (0, 0, 2, 0, 0), (1, 1, 0, 0, 0), (0, 1, 1, 0, 0),
    (1, 0, -3, 0, 0), (1, 0, -1, 0, 0), (1, 0, 2, 0, 0), (0, 0, -2, 0, -1), (1, 1, 1, 0, 0),
    (0, 1, -1, 0, -1), (0, 0, 3, 0, 2), (0, 1, -2, 0, -1), (0, 0, 1, 1, 1), (1, 1, -1, 1, 0),
    (0, 1, 2, 1, 1), (1, 1, -3, 0, -3), (1, 0, -4, 0, -3), (1, 0, 3, 0, 2), (1, 0, -2, 0, -1),
    (1, 0, 1, 1, 1), (1, 1, 3, 0, 2), (0, 0, -3, 0, -2), (0, 1, 3, 0, 3), (1, 1, 2, 1, 1),
    (0, 1, -3, 1, -2), (0, 0, 4, 0, 3), (1, 1, -2, 1, -1), (1, 1, -4, 0, -4), (0, 1, 4, 0, 3),
)
F32 = jnp.float32
BF16 = jnp.bfloat16


def make_kernel(ny, nz):
    nodes = 2 * ny
    feats_n = 4 * nz
    half = nz // 2
    last = nz - 1

    def kernel(feats, tiles_hbm, src, live, weight, bias, out,
               tiles, fbuf, own, psend, precv, rsend, rrecv, lsend, lrecv, xsend, xrecv, tsend, trecv,
               dloc, dsend, drecv, dtot, dxrecv,
               tsem, ag_s, ag_r, p_s, p_r, r_s, r_r, l_s, l_r, x_s, x_r, t_s, t_r,
               dr_s, dr_r, dx_s, dx_r):
        n = lax.axis_index("node")
        f = lax.axis_index("feat")
        z = f // 4
        h = (f // 2) % 2
        c = f % 2
        n_x = n + 1 - 2 * (n % 2)
        f_core = f + 1 - 2 * c
        f_opp = f + 2 - 4 * h
        f_up = (f + 4) % feats_n
        f_dn = (f + feats_n - 4) % feats_n
        f_up2 = (f + 8) % feats_n
        f_dn2 = (f + feats_n - 8) % feats_n

        def node_at(x, y):
            return ((n_x if x else n) + nodes + 2 * y) % nodes

        rows_n = tiles_hbm.shape[0]
        parts = tsem.shape[0]
        step_rows = rows_n // parts

        def tile_copy(i):
            sl = pl.ds(i * step_rows, step_rows)
            return pltpu.make_async_copy(tiles_hbm.at[sl], tiles.at[sl], tsem.at[i])

        for i in range(parts):
            tile_copy(i).start()

        barrier = pltpu.get_barrier_semaphore()
        steps = {((x - px) % 2, y - py) for _, x, y, px, py in HOPS}
        steps = sorted(steps | {(x, -y) for x, y in steps})
        near = [(node_at(x, y), f) for x, y in steps]
        near += [(n, fd) for fd in (f_core, f_opp, f_opp + 1 - 2 * c, f_up, f_dn, f_up2, f_dn2)]
        for nd, fd in near:
            pl.semaphore_signal(barrier, inc=1, device_id=dict(node=nd, feat=fd), device_id_type=MESH)
        pl.semaphore_wait(barrier, len(near))

        def remote(s, d, ss, rs, node=None, feat=None):
            dev = dict(node=n if node is None else node, feat=f if feat is None else feat)
            return pltpu.make_async_remote_copy(
                src_ref=s, dst_ref=d, send_sem=ss, recv_sem=rs, device_id=dev, device_id_type=MESH)

        def block_of(x, y):
            return ((n_x if x else n) + nodes - 2 * y) % nodes

        def hop(i):
            q, x, y, px, py = HOPS[i]
            block = block_of(px, py)
            rows = pl.ds(64 * q, 64)
            source = feats.at[rows] if (px, py) == (0, 0) else fbuf.at[block, rows]
            return remote(source, fbuf.at[block, rows], ag_s.at[i], ag_r.at[i], node=node_at((x - px) % 2, y - py))

        def landing(i):
            q, x, y, _, _ = HOPS[i]
            ref = fbuf.at[block_of(x, y), pl.ds(64 * q, 64)]
            return remote(ref, ref, ag_s.at[i], ag_r.at[i], node=n_x)

        def onward(q, x, y):
            for i in range(len(HOPS)):
                if HOPS[i][0] == q and HOPS[i][3:] == (x, y):
                    hop(i).start()

        for i in range(len(HOPS)):
            if HOPS[i][3:] == (0, 0):
                hop(i).start()

        fbuf[n] = feats[...]
        fbuf[nodes] = jnp.zeros_like(feats)
        dloc[...] = jnp.zeros_like(dloc)

        for i in range(len(HOPS)):
            landing(i).wait_recv()
            onward(*HOPS[i][:3])
        for i in range(parts):
            tile_copy(i).wait()

        slot_of = lax.broadcasted_iota(jnp.int32, (16, SLOTS * 128), 1) // 128

        def pair(u):
            return remote(psend.at[u], precv.at[u], p_s.at[u], p_r.at[u], feat=f_core)

        def group(u, j):
            off = jnp.where(u % 2 == 1, half - (u + 1) // 2, half + u // 2)
            zt = (z + off) % nz
            ht = j % 2
            ct = 1 - c if j < 2 else c
            r = 4 * zt + 2 * ht + ct
            count = live[0, r]
            a = jnp.concatenate([tiles[r, s] for s in range(SLOTS)], axis=1)
            b = jnp.concatenate(
                [fbuf[jnp.where(count > s, src[s, r], nodes)] for s in range(SLOTS)], axis=0)
            on = jnp.where(slot_of < count, 1.0, 0.0).astype(BF16)
            got = jnp.dot(a, b, preferred_element_type=F32)
            rowsum = lax.dot_general(on, a, (((1,), (1,)), ((), ())), preferred_element_type=F32)
            dloc[u, pl.ds(2 * ht + ct, 1), :] = rowsum[0:1, :]
            if j < 2:
                psend[u, ht] = got
            else:
                own[u, ht] = got
            if j == 1:
                pair(u).start()

        lanes0 = ((0, 0), (1, 1), (1, 0), (0, 1))
        lanes1 = ((0, LOW), (1, LOW))
        far = ((0, 0), (1, 1), (0, LOW))
        top = slice(0, TOP)
        low = slice(TOP, 128)

        def toward(w, k):
            if k % 2 == 0:
                return f_dn2 if w else f_up2
            return f_dn if w else f_up

        def ring(s, k):
            w, i = s
            if i is LOW:
                return remote(lsend.at[w, k], lrecv.at[w, k], l_s.at[w, k], l_r.at[w, k], feat=toward(w, k))
            return remote(rsend.at[w, i, k], rrecv.at[w, i, k], r_s.at[w, i, k], r_r.at[w, i, k], feat=toward(w, k))

        def dring(w, k):
            return remote(dsend.at[w, k], drecv.at[w, k], dr_s.at[w, k], dr_r.at[w, k], feat=toward(w, k))

        def cross(u):
            return remote(xsend.at[u], xrecv.at[u], x_s.at[u], x_r.at[u], feat=f_opp)

        def both(u, ht, rows):
            return own[u, ht, rows, :] + precv[u, ht, rows, :]

        def unit_of(w, k):
            return 0 if k == 0 else 2 * k - 1 + w

        def arrivals(s, k):
            if k % 2 or k == 0:
                return ()
            return (k - 1, k - 2) if k > 2 or s in far else (k - 1,)

        def arrived(s, k):
            w, i = s
            ring(s, k).wait_recv()
            return (lrecv[w, k] if i is LOW else rrecv[w, i, k]).astype(F32)

        def step(k, active):
            for s in active:
                w, i = s
                u = unit_of(w, k)
                v = both(u, i, top) if i is not LOW else both(u, h, low) + xrecv[u].astype(F32)
                for p in arrivals(s, k):
                    v = v + arrived(s, p)
                if i is not LOW:
                    rsend[w, i, k] = v.astype(BF16)
                else:
                    lsend[w, k] = v.astype(BF16)
                ring(s, k).start()

        def dstep(k):
            for w in range(1 if k == 0 else 2):
                v = dloc[unit_of(w, k)]
                for p in arrivals((0, 0) if w == 0 else (1, 0), k):
                    dring(w, p).wait_recv()
                    v = v + drecv[w, p]
                dsend[w, k] = v
                dring(w, k).start()

        def compute(lo, hi):
            def one(u, carry):
                for j in range(4):
                    group(u, j)
                return carry

            lax.fori_loop(lo, hi, one, 0)

        def send_cross(lo, hi):
            def one(u, carry):
                pair(u).wait_recv()
                xsend[u] = both(u, 1 - h, low).astype(BF16)
                cross(u).start()
                return carry

            lax.fori_loop(lo, hi, one, 0)

        def wait_cross(lo, hi):
            for u in range(lo, hi):
                cross(u).wait_recv()

        e = half - 1
        compute(0, 3)
        send_cross(0, 3)
        step(0, far[:2])
        step(1, lanes0)
        dstep(0)
        dstep(1)
        compute(3, 7)
        send_cross(3, 7)
        step(2, lanes0)
        step(3, lanes0)
        dstep(2)
        dstep(3)
        wait_cross(0, 3)
        step(0, far[2:])
        step(1, lanes1)
        compute(7, nz)
        send_cross(7, nz)
        step(4, lanes0)
        step(5, lanes0)
        dstep(4)
        dstep(5)
        wait_cross(3, 7)
        step(3, lanes1)
        step(2, lanes1)

        def total(i, v):
            for w in range(2):
                for p in (e, e - 1):
                    v = v + arrived((w, i), p)
            return v

        tail = remote(tsend, trecv, t_s, t_r, feat=f_opp)

        def dxc(i):
            return remote(dtot, dxrecv.at[i], dx_s.at[i], dx_r.at[i],
                          feat=(f_core, f_opp, f_opp + 1 - 2 * c)[i])

        tsend[...] = total(1 - h, both(last, 1 - h, top)).astype(BF16)
        tail.start()
        d = dloc[last]
        for w in range(2):
            for p in (e, e - 1):
                dring(w, p).wait_recv()
                d = d + drecv[w, p]
        dtot[...] = d
        for i in range(3):
            dxc(i).start()
        wait_cross(7, nz)
        step(5, lanes1)
        step(4, lanes1)
        kept = total(h, both(last, h, top))
        row = pl.ds(2 * h + c, 1)
        drow = dtot[row, :] + 1.0
        for i in range(3):
            dxc(i).wait_recv()
            drow = drow + dxrecv[i, row, :]
        inv = lax.rsqrt(jnp.broadcast_to(drow, (128, 128)).T)
        inv = jnp.concatenate([inv, inv], axis=1)

        def finish(rows, agg):
            mine = feats[rows, :].astype(F32)
            normed = ((agg + mine) * inv[rows, :]).astype(BF16)
            hidden = jnp.dot(normed, weight[...], preferred_element_type=F32) + bias[...]
            out[rows, :] = (mine + jnp.maximum(hidden, 0.0)).astype(BF16)

        tail.wait_recv()
        finish(top, kept + trecv[...].astype(F32))
        finish(low, total(LOW, both(last, h, low) + xrecv[last].astype(F32)))

        tail.wait_send()
        for i in range(len(HOPS)):
            hop(i).wait_send()
        for i in range(3):
            dxc(i).wait_send()
        def drain(u, carry):
            pair(u).wait_send()
            cross(u).wait_send()
            return carry

        lax.fori_loop(0, nz, drain, 0)

        for k in range(1, half):
            for s in lanes0 + lanes1:
                ring(s, k).wait_send()
            dring(0, k).wait_send()
            dring(1, k).wait_send()
        for s in far:
            ring(s, 0).wait_send()
        dring(0, 0).wait_send()

    return kernel


def make_body(ny, nz):
    nodes = 2 * ny
    half = nz // 2
    dma = pltpu.SemaphoreType.DMA
    vmem = pl.BlockSpec(memory_space=pltpu.VMEM)
    smem = pl.BlockSpec(memory_space=pltpu.SMEM)

    def body(feats, tile_values, source_group, live_slots, proj_weight, proj_bias):
        rows_n = tile_values.shape[0]
        scratch = [
            pltpu.VMEM((rows_n, SLOTS, 128, 128), BF16),
            pltpu.VMEM((nodes + 1, 128, 256), BF16),
            pltpu.VMEM((nz, 2, 128, 256), F32),
            pltpu.VMEM((nz, 2, 128, 256), F32),
            pltpu.VMEM((nz, 2, 128, 256), F32),
            pltpu.VMEM((2, 2, half, TOP, 256), BF16),
            pltpu.VMEM((2, 2, half, TOP, 256), BF16),
            pltpu.VMEM((2, half, 128 - TOP, 256), BF16),
            pltpu.VMEM((2, half, 128 - TOP, 256), BF16),
            pltpu.VMEM((nz, 128 - TOP, 256), BF16),
            pltpu.VMEM((nz, 128 - TOP, 256), BF16),
            pltpu.VMEM((TOP, 256), BF16),
            pltpu.VMEM((TOP, 256), BF16),
            pltpu.VMEM((nz, 8, 128), F32),
            pltpu.VMEM((2, half, 8, 128), F32),
            pltpu.VMEM((2, half, 8, 128), F32),
            pltpu.VMEM((8, 128), F32),
            pltpu.VMEM((3, 8, 128), F32),
            dma((6,)),
            dma((len(HOPS),)), dma((len(HOPS),)),
            dma((nz,)), dma((nz,)),
            dma((2, 2, half)), dma((2, 2, half)),
            dma((2, half)), dma((2, half)),
            dma((nz,)), dma((nz,)),
            dma, dma,
            dma((2, half)), dma((2, half)),
            dma((3,)), dma((3,)),
        ]
        return pl.pallas_call(
            make_kernel(ny, nz),
            out_shape=jax.ShapeDtypeStruct(feats.shape, BF16),
            in_specs=[vmem, pl.BlockSpec(memory_space=pl.ANY), smem, smem, vmem, vmem],
            out_specs=vmem,
            scratch_shapes=scratch,
            compiler_params=pltpu.CompilerParams(
                collective_id=0, has_side_effects=True, vmem_limit_bytes=60 << 20),
            name="graph_layer",
        )(feats, tile_values, source_group.T, live_slots.T, proj_weight, proj_bias.reshape(1, -1))

    return body


def solution(mesh):
    placed = (
        P(("node", "feat"), None),
        P("node", "feat", None, None),
        P("node", "feat"),
        P("node", "feat"),
        P(),
        P(),
    )
    return jax.shard_map(
        make_body(mesh.shape["node"] // 2, mesh.shape["feat"] // 4),
        mesh=mesh, in_specs=placed, out_specs=P(("node", "feat"), None), check_vma=False,
    )
```

time: 68.2 us -> 61.6 us (0.903)
  Pallas kernels: 66.5 us -> 59.9 us
    pallas_call x1, Pallas kernels: 66.5 us -> 59.9 us  [body(): pl.pallas_call(make_kernel(ny, nz), out_shape=jax.ShapeDtypeStruct(feats....]
where the time goes in v3:
time: 61.6 us; the launch traced here: 61.4 us
  Pallas kernels  59.9 us (97%)
  local copies, waits for them, and re-layouts  1.47 us (2%)
    pallas_call x1, Pallas kernels, body(): pl.pallas_call(make_kernel(ny, nz), out_shape=jax.ShapeDtypeStruct(feats....  59.9 us
    unnamed x1, local copies, waits for them, and re-layouts  1.47 us

profile of v3, /device:TPU:1, one launch (start us, length us, event | category | flops | bytes accessed | tf_op | source)
XLA Modules:
  0.0 61.4 jit_solution(13174727023187859870)
XLA Ops:
  0.0 59.9 %graph_layer.1 = bf16[128,256]{1,0:T(8,128)(2,1)} custom-call(bf16[128,256]{1,0:T(8,128)(2,1)} %feats.1, bf16[48,3,128,128]{3,2,1,0:T(8,128)(2,1)} %tiles_hbm.1, s32[3,48]{1,0:T(4,128)} %bitcast.3, s32[1,48]{1,0:T(1,128)} %bitcast.5, bf16[256,256]{1,0:T(8,128)(2,1)} %weight.1, f32[1,256]{1,0:T(1,128)} %bitcast.4), custom_call_target="tpu_custom_call" | custom-call | tf_op jit(solution)/shard_map/graph_layer/pallas_call | solution.py:350
  59.9 1.5 %copy.8 = bf16[128,256]{1,0:T(8,128)(2,1)} copy(bf16[128,256]{1,0:T(8,128)(2,1)} %graph_layer.1) | data formatting | bytes 131072

commit v4 on v3

--- a/solution.py
+++ b/solution.py
@@ -6,7 +6,7 @@
 from jax.sharding import PartitionSpec as P
 
 SLOTS = 3
-TOP = 48
+TOP = 32
 LOW = "low"
 MESH = pl.DeviceIdType.MESH
 HOPS = (
@@ -176,7 +176,11 @@
             for s in active:
                 w, i = s
                 u = unit_of(w, k)
-                v = both(u, i, top) if i is not LOW else both(u, h, low) + xrecv[u].astype(F32)
+                if i is LOW:
+                    cross(u).wait_recv()
+                    v = both(u, h, low) + xrecv[u].astype(F32)
+                else:
+                    v = both(u, i, top)
                 for p in arrivals(s, k):
                     v = v + arrived(s, p)
                 if i is not LOW:
@@ -210,10 +214,6 @@
                 return carry
 
             lax.fori_loop(lo, hi, one, 0)
-
-        def wait_cross(lo, hi):
-            for u in range(lo, hi):
-                cross(u).wait_recv()
 
         e = half - 1
         compute(0, 3)
@@ -228,7 +228,6 @@
         step(3, lanes0)
         dstep(2)
         dstep(3)
-        wait_cross(0, 3)
         step(0, far[2:])
         step(1, lanes1)
         compute(7, nz)
@@ -237,7 +236,6 @@
         step(5, lanes0)
         dstep(4)
         dstep(5)
-        wait_cross(3, 7)
         step(3, lanes1)
         step(2, lanes1)
 
@@ -263,7 +261,6 @@
         dtot[...] = d
         for i in range(3):
             dxc(i).start()
-        wait_cross(7, nz)
         step(5, lanes1)
         step(4, lanes1)
         kept = total(h, both(last, h, top))
@@ -283,6 +280,7 @@
 
         tail.wait_recv()
         finish(top, kept + trecv[...].astype(F32))
+        cross(last).wait_recv()
         finish(low, total(LOW, both(last, h, low) + xrecv[last].astype(F32)))
 
         tail.wait_send()

time: 61.6 us -> 59.2 us (0.961)
  Pallas kernels: 59.9 us -> 57.5 us
    pallas_call x1, Pallas kernels: 59.9 us -> 57.5 us  [body(): pl.pallas_call(make_kernel(ny, nz), out_shape=jax.ShapeDtypeStruct(feats....]
where the time goes in v4:
time: 59.2 us; the launch traced here: 59 us
  Pallas kernels  57.5 us (97%)
  local copies, waits for them, and re-layouts  1.47 us (2%)
    pallas_call x1, Pallas kernels, body(): pl.pallas_call(make_kernel(ny, nz), out_shape=jax.ShapeDtypeStruct(feats....  57.5 us
    unnamed x1, local copies, waits for them, and re-layouts  1.47 us

profile of v4, /device:TPU:1, one launch (start us, length us, event | category | flops | bytes accessed | tf_op | source)
XLA Modules:
  0.0 59.0 jit_solution(7170435783765101877)
XLA Ops:
  0.0 57.5 %graph_layer.1 = bf16[128,256]{1,0:T(8,128)(2,1)} custom-call(bf16[128,256]{1,0:T(8,128)(2,1)} %feats.1, bf16[48,3,128,128]{3,2,1,0:T(8,128)(2,1)} %tiles_hbm.1, s32[3,48]{1,0:T(4,128)} %bitcast.3, s32[1,48]{1,0:T(1,128)} %bitcast.5, bf16[256,256]{1,0:T(8,128)(2,1)} %weight.1, f32[1,256]{1,0:T(1,128)} %bitcast.4), custom_call_target="tpu_custom_call" | custom-call | tf_op jit(solution)/shard_map/graph_layer/pallas_call | solution.py:348
  57.5 1.5 %copy.8 = bf16[128,256]{1,0:T(8,128)(2,1)} copy(bf16[128,256]{1,0:T(8,128)(2,1)} %graph_layer.1) | data formatting | bytes 131072

commit v5 on v4

--- a/solution.py
+++ b/solution.py
@@ -224,18 +224,18 @@
         dstep(1)
         compute(3, 7)
         send_cross(3, 7)
+        dstep(3)
         step(2, lanes0)
         step(3, lanes0)
         dstep(2)
-        dstep(3)
         step(0, far[2:])
         step(1, lanes1)
         compute(7, nz)
         send_cross(7, nz)
+        dstep(5)
         step(4, lanes0)
+        dstep(4)
         step(5, lanes0)
-        dstep(4)
-        dstep(5)
         step(3, lanes1)
         step(2, lanes1)
 
@@ -251,8 +251,6 @@
             return remote(dtot, dxrecv.at[i], dx_s.at[i], dx_r.at[i],
                           feat=(f_core, f_opp, f_opp + 1 - 2 * c)[i])
 
-        tsend[...] = total(1 - h, both(last, 1 - h, top)).astype(BF16)
-        tail.start()
         d = dloc[last]
         for w in range(2):
             for p in (e, e - 1):
@@ -261,6 +259,8 @@
         dtot[...] = d
         for i in range(3):
             dxc(i).start()
+        tsend[...] = total(1 - h, both(last, 1 - h, top)).astype(BF16)
+        tail.start()
         step(5, lanes1)
         step(4, lanes1)
         kept = total(h, both(last, h, top))

time: 59.2 us -> 59.3 us (level)
  no operation moved by 1% of the time
where the time goes in v5:
time: 59.3 us; the launch traced here: 59.1 us
  Pallas kernels  57.6 us (97%)
  local copies, waits for them, and re-layouts  1.47 us (2%)
    pallas_call x1, Pallas kernels, body(): pl.pallas_call(make_kernel(ny, nz), out_shape=jax.ShapeDtypeStruct(feats....  57.6 us
    unnamed x1, local copies, waits for them, and re-layouts  1.47 us

profile of v5, /device:TPU:1, one launch (start us, length us, event | category | flops | bytes accessed | tf_op | source)
XLA Modules:
  0.0 59.1 jit_solution(14501757518944099511)
XLA Ops:
  0.0 57.6 %graph_layer.1 = bf16[128,256]{1,0:T(8,128)(2,1)} custom-call(bf16[128,256]{1,0:T(8,128)(2,1)} %feats.1, bf16[48,3,128,128]{3,2,1,0:T(8,128)(2,1)} %tiles_hbm.1, s32[3,48]{1,0:T(4,128)} %bitcast.3, s32[1,48]{1,0:T(1,128)} %bitcast.5, bf16[256,256]{1,0:T(8,128)(2,1)} %weight.1, f32[1,256]{1,0:T(1,128)} %bitcast.4), custom_call_target="tpu_custom_call" | custom-call | tf_op jit(solution)/shard_map/graph_layer/pallas_call | solution.py:348
  57.7 1.5 %copy.8 = bf16[128,256]{1,0:T(8,128)(2,1)} copy(bf16[128,256]{1,0:T(8,128)(2,1)} %graph_layer.1) | data formatting | bytes 131072
